TPU v7x, 32 devices: a whole 2x2x4 slice. The times are simulated.
32 devices in a mesh: req: 8 (over z, y), tp: 4 (over x, core).
Axes of the slice: x: 2, y: 2, z: 4, core: 2. Of those that a mesh axis runs over, the one named last changes fastest.
Arguments:
- tokens: bfloat16 [4096, 2048], P('req')
- token_request_number: int32 [8, 512], P('req'), may hold values from 0 to 7, never falling along the last dimension, each value on 1 to 256 neighbouring positions
- request_adapter_position: int32 [8, 8], P('req'), may hold values from 0 to 15
- adapters_in_use: int32 [16], replicated, may hold values from 0 to 15, as said below
- adapter_storage_slot: int32 [16], replicated, may hold values from 0 to 15, each once
- input_norm_gain: bfloat16 [2048], replicated, may hold values from 0.5 to 1.5
- query_weight: bfloat16 [2048, 2048], P('req', 'tp')
- key_weight: bfloat16 [2048, 2048], P('req', 'tp')
- value_weight: bfloat16 [2048, 2048], P('req', 'tp'), may hold values from -0.125 to 0.125
- output_weight: bfloat16 [2048, 2048], P('tp', 'req'), may hold values from -0.125 to 0.125
- adapter_down_weight: bfloat16 [16, 2, 16, 2048], P('req'), may hold values from -0.125 to 0.125
- adapter_up_weight: bfloat16 [16, 2, 16, 2048], P('req', None, None, 'tp'), may hold values from -0.75 to 0.75
Outputs:
- layer_out: bfloat16 [4096, 2048], P('req', 'tp')
Inputs may be any that keep to these rules, and one draw needn't show every extreme that they name: `adapters_in_use`: 16 different adapter numbers; 0 and 15 are always among them. `token_request_number`: the 512 tokens of each index of req form exactly 8 requests in order, each of 1 to 256 tokens, and one of exactly 256.
All inputs are finite; a program needn't handle non-finite values.
Results may differ from a plain program's by a relative error of at most 0.01.
Values may be sent and summed in bfloat16 or wider, within the bound.
A program may use at most 64 MiB of HBM per device.

v0:
```python
import jax
import jax.numpy as jnp
from jax import lax
from jax.sharding import PartitionSpec as P

HEAD_WIDTH = 64
norm_eps = 1e-05
rope_base = 130000.0
adapter_scale = 2.0


def fetch_adapters(down_part, up_part, active_slots, request_adapters, req_total):
    slot_total = down_part.shape[0]
    stored = jnp.concatenate([down_part, up_part], axis=1)
    split = down_part.shape[1]
    if slot_total * req_total <= 2 * active_slots.shape[0]:
        fetched = lax.all_gather(stored, "req", axis=0, tiled=True)
        places = active_slots[request_adapters]
    else:
        own = active_slots // slot_total == lax.axis_index("req")
        rows = jnp.where(
            own[:, None],
            jnp.take(stored, active_slots % slot_total, axis=0),
            jnp.zeros((), stored.dtype),
        )
        fetched = lax.psum(rows, "req")
        places = request_adapters
    return (fetched[:, :split], fetched[:, split:], places)


def positions_of(segment):
    ordinal = jnp.arange(segment.shape[0], dtype=jnp.int32)
    starts = jnp.concatenate([jnp.ones((1,), jnp.bool_), segment[1:] != segment[:-1]])
    segment_start = lax.cummax(jnp.where(starts, ordinal, jnp.zeros_like(ordinal)), axis=0)
    return ordinal - segment_start


def apply_rotation(values, token_positions):
    half_dim = HEAD_WIDTH // 2
    frequency = rope_base ** (-(jnp.arange(half_dim, dtype=jnp.float32) * 2.0 / HEAD_WIDTH))
    angles = token_positions.astype(jnp.float32)[:, None] * frequency[None, :]
    cosine = jnp.cos(angles)[:, None, :]
    sine_part = jnp.sin(angles)[:, None, :]
    first_half = values[..., :half_dim]
    second_half = values[..., half_dim:]
    return jnp.concatenate(
        [
            first_half * cosine - second_half * sine_part,
            second_half * cosine + first_half * sine_part,
        ],
        axis=-1,
    )


def attend(query_per_head, key_heads, value_per_head, segment):
    scores = (
        jnp.einsum("qhd,khd->hqk", query_per_head, key_heads, preferred_element_type=jnp.float32)
        * 0.125
    )
    ordinal = jnp.arange(segment.shape[0], dtype=jnp.int32)
    allowed = (segment[:, None] == segment[None, :]) & (ordinal[None, :] <= ordinal[:, None])
    scores = jnp.where(allowed[None], scores, jnp.float32(-1e30))
    row_peak = jnp.max(scores, axis=-1, keepdims=True)
    exponent = jnp.where(allowed[None], jnp.exp(scores - row_peak), jnp.float32(0.0))
    weights = (exponent / jnp.sum(exponent, axis=-1, keepdims=True)).astype(jnp.bfloat16)
    return jnp.einsum(
        "hqk,khd->qhd", weights, value_per_head, preferred_element_type=jnp.float32
    ).astype(jnp.bfloat16)


def local(
    tokens,
    token_request_number,
    request_adapter_position,
    adapters_in_use,
    adapter_storage_slot,
    input_norm_gain,
    query_weight,
    key_weight,
    value_weight,
    output_weight,
    adapter_down_weight,
    adapter_up_weight,
):
    row_total, model_width = tokens.shape
    local_width = query_weight.shape[1]
    reduced_rows = adapter_down_weight.shape[2]
    active_count = adapters_in_use.shape[0]
    slot_total = adapter_down_weight.shape[0]
    segment = token_request_number[0]
    request_adapters = request_adapter_position[0]
    tp_total = lax.axis_size("tp")
    req_total = lax.axis_size("req")
    part_rows = reduced_rows // tp_total
    down_part = lax.dynamic_slice_in_dim(
        adapter_down_weight, lax.axis_index("tp") * part_rows, part_rows, 2
    ).reshape(slot_total, 2 * part_rows * model_width)
    up_part = adapter_up_weight.reshape(slot_total, 2 * reduced_rows * local_width)
    down_all, up_all, request_places = fetch_adapters(
        down_part,
        up_part,
        jnp.take(adapter_storage_slot, adapters_in_use, axis=0),
        request_adapters,
        req_total,
    )
    place_total = down_all.shape[0]
    floats = tokens.astype(jnp.float32)
    normed = (
        floats
        * lax.rsqrt(jnp.mean(floats * floats, axis=-1, keepdims=True) + norm_eps)
        * input_norm_gain.astype(jnp.float32)
    ).astype(jnp.bfloat16)
    query_plain = jnp.dot(
        normed,
        lax.all_gather(query_weight, "req", axis=0, tiled=True),
        preferred_element_type=jnp.float32,
    )
    key_base = jnp.dot(
        normed,
        lax.all_gather(key_weight, "req", axis=0, tiled=True),
        preferred_element_type=jnp.float32,
    )
    value_plain = jnp.dot(
        normed,
        lax.all_gather(value_weight, "req", axis=0, tiled=True),
        preferred_element_type=jnp.float32,
    )
    request_total = request_adapters.shape[0]
    member = segment[:, None] == jnp.arange(request_total, dtype=jnp.int32)[None, :]
    token_place = jnp.sum(
        jnp.where(member, request_places[None, :], jnp.zeros_like(request_places)[None, :]), axis=1
    )
    share = 2 * part_rows
    shrunk_all = lax.dot_general(
        normed,
        down_all.reshape(place_total * share, model_width),
        (((1,), (1,)), ((), ())),
        preferred_element_type=jnp.float32,
    ).astype(jnp.bfloat16)
    column = jnp.arange(place_total * share, dtype=jnp.int32)
    kept = jnp.where(
        token_place[:, None] == (column // share)[None, :], shrunk_all, jnp.zeros((), jnp.bfloat16)
    )
    fold = (column % share)[:, None] == jnp.arange(share, dtype=jnp.int32)[None, :]
    shrunk_part = jnp.dot(
        kept, fold.astype(jnp.bfloat16), preferred_element_type=jnp.float32
    ).astype(jnp.bfloat16)
    shrunk = lax.all_gather(shrunk_part, "tp", axis=1, tiled=True)
    source = jnp.arange(tp_total * share, dtype=jnp.int32)
    source_kind = source % share // part_rows
    source_rank = source // share * part_rows + source % part_rows
    target = jnp.arange(place_total * reduced_rows, dtype=jnp.int32)
    mine = token_place[:, None] == (target // reduced_rows)[None, :]
    up_all = up_all.reshape(place_total, 2, reduced_rows, local_width)

    def change_of(kind):
        spread_map = (source_kind == kind)[:, None] & (
            source_rank[:, None] == (target % reduced_rows)[None, :]
        )
        spread = jnp.dot(
            shrunk, spread_map.astype(jnp.bfloat16), preferred_element_type=jnp.float32
        ).astype(jnp.bfloat16)
        spread = jnp.where(mine, spread, jnp.zeros((), jnp.bfloat16))
        return jnp.dot(
            spread,
            up_all[:, kind].reshape(place_total * reduced_rows, local_width),
            preferred_element_type=jnp.float32,
        )

    query_change = change_of(0)
    value_change = change_of(1)
    head_total = local_width // HEAD_WIDTH
    token_positions = positions_of(segment)
    query_per_head = apply_rotation(
        (query_plain + adapter_scale * query_change).reshape(row_total, head_total, HEAD_WIDTH),
        token_positions,
    ).astype(jnp.bfloat16)
    key_heads = apply_rotation(
        key_base.reshape(row_total, head_total, HEAD_WIDTH), token_positions
    ).astype(jnp.bfloat16)
    value_per_head = (
        (value_plain + adapter_scale * value_change)
        .astype(jnp.bfloat16)
        .reshape(row_total, head_total, HEAD_WIDTH)
    )
    attended = attend(query_per_head, key_heads, value_per_head, segment).reshape(
        row_total, local_width
    )
    partial_out = jnp.dot(
        attended,
        lax.all_gather(output_weight, "req", axis=1, tiled=True),
        preferred_element_type=jnp.float32,
    )
    summed = lax.psum_scatter(
        partial_out.astype(jnp.bfloat16), "tp", scatter_dimension=1, tiled=True
    ).astype(jnp.float32)
    share_width = summed.shape[1]
    residual_part = lax.dynamic_slice_in_dim(
        tokens, lax.axis_index("tp") * share_width, share_width, 1
    )
    return (summed + residual_part.astype(jnp.float32)).astype(jnp.bfloat16)


def solution(mesh):
    in_specs = (
        P("req", None),
        P("req", None),
        P("req", None),
        P(),
        P(),
        P(),
        P("req", "tp"),
        P("req", "tp"),
        P("req", "tp"),
        P("tp", "req"),
        P("req", None, None, None),
        P("req", None, None, "tp"),
    )
    out_specs = P("req", "tp")
    return jax.shard_map(local, mesh=mesh, in_specs=in_specs, out_specs=out_specs, check_vma=False)
```

profile of v0, /device:TPU:0, one launch (start us, length us, event | category | flops | bytes accessed | tf_op | source)
XLA Modules:
  0.0 296.7 jit_solution(14154784594400048160)
XLA Ops:
  6.6 1.0 copy.18
  12.0 2.1 fusion.2
  15.6 0.9 fusion.18
  17.9 0.9 multiply_cosine_fusion
  18.9 33.5 %all-gather.15.cloned.1.call-done = bf16[8,2,32768]{2,1,0:T(2,128)(2,1)} async-done(((bf16[1,2,32768]{2,1,0:T(2,128)(2,1)}), bf16[8,2,32768]{2,1,0:T(2,128)(2,1)}) %all-gather.15.cloned.1.call-update) | async-done | bytes 1048592 | tf_op jit(solution)/shard_map/all_gather | solution.py:17
  52.4 1.5 reshape.319
  55.8 1.3 reshape.294
  57.0 0.9 fusion.17
  58.0 5.4 %all_gather.20 = bf16[512,32]{0,1:T(8,128)(2,1)S(1)} all-gather(bf16[512,8]{0,1:T(8,128)(2,1)S(1)} %fusion.17), channel_id=1, replica_groups=mesh['req'=8,'tp'=4] {'tp'}, dimensions={1}, use_global_device_ids=true | all-gather | bytes 40960 | tf_op jit(solution)/shard_map/all_gather | solution.py:148
  63.4 39.2 %all-gather.7.cloned.1.call-done = bf16[2048,512]{1,0:T(8,128)(2,1)} async-done(((bf16[256,512]{1,0:T(8,128)(2,1)}), bf16[2048,512]{1,0:T(8,128)(2,1)}) %all-gather.7.cloned.1.call-update) | async-done | bytes 2097168 | tf_op jit(solution)/shard_map/all_gather | solution.py:125
  102.6 3.0 %fusion.68 = f32[512,512]{0,1:T(8,128)S(1)} fusion(bf16[2048,512]{1,0:T(8,128)(2,1)} %all-gather.7.cloned.1.call-done, bf16[512,2048]{1,0:T(8,128)(2,1)S(1)} %copy-done.2, f32[2048]{0:T(1024)S(1)} %convert_element_type.59, f32[512]{0:T(512)S(1)} %add_rsqrt_fusion), kind=kOutput, calls=%fused_computation.120 | convolution fusion | flops 1077936128 | bytes 5253120 | tf_op jit(solution)/shard_map/dot_general | solution.py:123
  105.6 2.3 fusion.12
  107.9 44.7 %all-gather.9.cloned.1.call-done = bf16[2048,512]{1,0:T(8,128)(2,1)} async-done(((bf16[256,512]{1,0:T(8,128)(2,1)}), bf16[2048,512]{1,0:T(8,128)(2,1)}) %all-gather.9.cloned.1.call-update) | async-done | bytes 2097168 | tf_op jit(solution)/shard_map/all_gather | solution.py:115
  152.5 3.9 %fusion.64 = f32[512,512]{0,1:T(8,128)} fusion(bf16[2048,512]{1,0:T(8,128)(2,1)} %all-gather.9.cloned.1.call-done, bf16[512,2048]{1,0:T(8,128)(2,1)S(1)} %copy-done.2, f32[2048]{0:T(1024)S(1)} %convert_element_type.59, f32[512]{0:T(512)S(1)} %add_rsqrt_fusion), kind=kOutput, calls=%fused_computation.119 | convolution fusion | flops 1077936128 | bytes 5253120 | tf_op jit(solution)/shard_map/dot_general | solution.py:113
  156.5 1.9 fusion.9
  158.4 44.0 %all-gather.11.cloned.1.call-done = bf16[2048,512]{1,0:T(8,128)(2,1)} async-done(((bf16[256,512]{1,0:T(8,128)(2,1)}), bf16[2048,512]{1,0:T(8,128)(2,1)}) %all-gather.11.cloned.1.call-update) | async-done | bytes 2097168 | tf_op jit(solution)/shard_map/all_gather | solution.py:120
  202.3 3.0 %fusion.62 = f32[512,512]{0,1:T(8,128)S(1)} fusion(bf16[2048,512]{1,0:T(8,128)(2,1)} %all-gather.11.cloned.1.call-done, bf16[512,2048]{1,0:T(8,128)(2,1)S(1)} %copy-done.2, f32[2048]{0:T(1024)S(1)} %convert_element_type.59, f32[512]{0:T(512)S(1)} %add_rsqrt_fusion), kind=kOutput, calls=%fused_computation.118 | convolution fusion | flops 1077936128 | bytes 5253120 | tf_op jit(solution)/shard_map/dot_general | solution.py:118
  205.4 1.3 subtract_convert_fusion.1
  206.7 8.2 %fusion.72 = (f32[8,512]{1,0:T(8,128)S(1)}, f32[8,512,512]{1,2,0:T(8,128)}) fusion(pred[512,512]{0,1:T(8,128)(4,1)} %fusion.18, bf16[512,8,32]{0,2,1:T(8,128)(2,1)} %get-tuple-element.13, bf16[512,8,32]{0,2,1:T(8,128)(2,1)} %get-tuple-element.14, bf16[512,8,32]{0,2,1:T(8,128)(2,1)} %get-tuple-element.6, bf16[512,8,32]{0,2,1:T(8,128)(2,1)} %get-tuple-element.5), kind=kOutput, calls=%fused_computation.123 | convolution fusion | flops 281018880 | bytes 9715712 | tf_op jit(solution)/shard_map/sub | solution.py:64
  214.9 4.3 %fusion.11 = bf16[8,64,512]{2,1,0:T(8,128)(2,1)S(1)} fusion(bf16[512,8,64]{0,2,1:T(8,128)(2,1)S(1)} %bitcast.46, f32[8,512,512]{1,2,0:T(8,128)} %get-tuple-element.18, f32[8,512]{1,0:T(8,128)S(1)} %get-tuple-element.17), kind=kOutput, calls=%fused_computation.21 | convolution fusion | flops 272891904 | bytes 9453568 | tf_op jit(solution)/shard_map/hqk,khd->qhd/dot_general | solution.py:66
  219.2 34.7 %all-gather.13.cloned.1.call-done = bf16[512,2048]{1,0:T(8,128)(2,1)} async-done(((bf16[512,256]{1,0:T(8,128)(2,1)}), bf16[512,2048]{1,0:T(8,128)(2,1)}) %all-gather.13.cloned.1.call-update) | async-done | bytes 2097168 | tf_op jit(solution)/shard_map/all_gather | solution.py:191
  253.8 4.2 %convolution_convert_fusion = bf16[512,2048]{1,0:T(8,128)(2,1)} fusion(bf16[512,512]{0,1:T(8,128)(2,1)S(1)} %bitcast.51, bf16[512,2048]{1,0:T(8,128)(2,1)} %all-gather.13.cloned.1.call-done), kind=kOutput, calls=%fused_computation.16 | convolution fusion | flops 1074790400 | bytes 4718592 | tf_op jit(solution)/shard_map/dot_general | solution.py:189
  258.1 29.8 %reduce-scatter.2.cloned.1.call-done = bf16[512,512]{1,0:T(8,128)(2,1)} async-done(((bf16[512,2048]{1,0:T(8,128)(2,1)}), bf16[512,512]{1,0:T(8,128)(2,1)}) %reduce-scatter.2.cloned.1.call-update) | async-done | bytes 524304 | tf_op jit(solution)/shard_map/reduce_scatter | solution.py:194
  287.8 2.0 add_convert_fusion
  (57 shorter events, 9.1 us)
Async XLA Ops:
  6.5 1.1 copy-start
  6.5 8.9 %copy-start.6 = (s32[16]{0:T(128)S(1)}, s32[16]{0:T(128)}, u32[]{:S(2)}) copy-start(s32[16]{0:T(128)} %param.15) | copy-start | bytes 196
  6.5 8.2 %copy-start.1 = (s32[16]{0:T(128)S(1)}, s32[16]{0:T(128)}, u32[]{:S(2)}) copy-start(s32[16]{0:T(128)} %param.16) | copy-start | bytes 196
  6.5 8.9 %copy-start.7 = (s32[1,8]{1,0:T(1,128)S(1)}, s32[1,8]{1,0:T(1,128)}, u32[]{:S(2)}) copy-start(s32[1,8]{1,0:T(1,128)} %param.14) | copy-start | bytes 100
  6.5 8.9 %copy-start.5 = (s32[1,512]{1,0:T(1,128)S(1)}, s32[1,512]{1,0:T(1,128)}, u32[]{:S(2)}) copy-start(s32[1,512]{1,0:T(1,128)} %param.13) | copy-start | bytes 6148
  6.5 45.8 %all-gather.15.cloned.1.call-start = ((), (), s32[]{:S(2)}) async-start(), calls=%async_computation.6 | async-start | bytes 1179648 | tf_op jit(solution)/shard_map/all_gather | solution.py:17
  8.5 94.1 %all-gather.7.cloned.1.call-start = ((), (), s32[]{:S(2)}) async-start(), calls=%async_computation.1 | async-start | bytes 2359296 | tf_op jit(solution)/shard_map/all_gather | solution.py:125
  9.3 143.3 %all-gather.9.cloned.1.call-start = ((), (), s32[]{:S(2)}) async-start(), calls=%async_computation.2 | async-start | bytes 2359296 | tf_op jit(solution)/shard_map/all_gather | solution.py:115
  10.0 192.3 %all-gather.11.cloned.1.call-start = ((), (), s32[]{:S(2)}) async-start(), calls=%async_computation.3 | async-start | bytes 2359296 | tf_op jit(solution)/shard_map/all_gather | solution.py:120
  10.6 243.2 %all-gather.13.cloned.1.call-start = ((), (), s32[]{:S(2)}) async-start(), calls=%async_computation.4 | async-start | bytes 2359296 | tf_op jit(solution)/shard_map/all_gather | solution.py:191
  11.2 276.6 %reduce-scatter.2.cloned.1.call-start = ((), (), s32[]{:S(2)}) async-start(), calls=%async_computation.5 | async-start | bytes 2621440 | tf_op jit(solution)/shard_map/reduce_scatter | solution.py:194
  15.4 41.6 %copy-start.2 = (bf16[512,2048]{1,0:T(8,128)(2,1)S(1)}, bf16[512,2048]{1,0:T(8,128)(2,1)}, u32[]{:S(2)}) copy-start(bf16[512,2048]{1,0:T(8,128)(2,1)} %param.12) | copy-start | bytes 6291460
  202.3 3.0 %copy-start.4 = (f32[512,32]{0,1:T(8,128)S(1)}, f32[512,32]{0,1:T(8,128)}, u32[]{:S(2)}) copy-start(f32[512,32]{0,1:T(8,128)} %get-tuple-element.16) | copy-start | bytes 196612
  206.7 8.2 %copy-start.3 = (bf16[512,512]{0,1:T(8,128)(2,1)S(1)}, bf16[512,512]{0,1:T(8,128)(2,1)}, u32[]{:S(2)}) copy-start(bf16[512,512]{0,1:T(8,128)(2,1)} %fusion.12) | copy-start | bytes 1572868
Sparse Core Ops, SparseCore 0:
  9.5 42.8 all-gather.14
  54.5 48.0 all-gather.6
  104.7 47.7 all-gather.8
  154.5 47.7 all-gather.10
  204.2 49.5 all-gather.12
  258.2 29.5 reduce-scatter.1
where the time goes:
time: 297 us
  waiting for transfers between devices  228 us (77%)
  matrix products  31.7 us (11%)
  between operations  13.7 us (5%)
  other arithmetic  10.1 us (3%)
  local copies, waits for them, and re-layouts  7.27 us (2%)
  blocking collectives  5.39 us (2%)
    all_gather x1, waiting for transfers between devices, local(): lax.all_gather(query_weight, 'req', axis=0, tiled=True)  44.7 us
    all_gather x1, waiting for transfers between devices, local(): lax.all_gather(key_weight, 'req', axis=0, tiled=True)  44 us
    all_gather x1, waiting for transfers between devices, local(): lax.all_gather(value_weight, 'req', axis=0, tiled=True)  39.2 us
    all_gather x1, waiting for transfers between devices, local(): lax.all_gather(output_weight, 'req', axis=1, tiled=True)  34.7 us
    all_gather x1, waiting for transfers between devices, fetch_adapters(): fetched = lax.all_gather(stored, 'req', axis=0, tiled=True)  33.5 us
    reduce_scatter x1, waiting for transfers between devices, local(): lax.psum_scatter(partial_out.astype(jnp.bfloat16), 'tp', scatter_dimensio...  29.8 us
    sub x1, matrix products, attend(): scores - row_peak  8.2 us
  transfers between devices with their start and end apart: 6, of which 6 were waited for; matrix products, arithmetic and copies ran while one was open for 14% of the time, Pallas kernels for 0%

commit v1 on v0

--- a/solution.py
+++ b/solution.py
@@ -14,7 +14,14 @@
     stored = jnp.concatenate([down_part, up_part], axis=1)
     split = down_part.shape[1]
     if slot_total * req_total <= 2 * active_slots.shape[0]:
-        fetched = lax.all_gather(stored, "req", axis=0, tiled=True)
+        ring = [stored]
+        for hop in range(7):
+            ring.append(lax.ppermute(ring[-1], "req", [(dev, (dev + 1) % 8) for dev in range(8)]))
+        fetched = jnp.roll(
+            jnp.concatenate(ring[::-1], axis=0),
+            (lax.axis_index("req") + 1) * ring[0].shape[0],
+            axis=0,
+        )
         places = active_slots[request_adapters]
     else:
         own = active_slots // slot_total == lax.axis_index("req")

time: 297 us -> 266 us (0.90)
  waiting for transfers between devices: 228 us -> 195 us
  starting transfers between devices: 0.23 us -> 3.23 us
    ppermute x0 -> x7, waiting for transfers between devices: none -> 56 us  [fetch_adapters(): lax.ppermute(ring[-1], 'req', [(dev, (dev + 1) % 8) for dev in range(8)])]
    all_gather x1, waiting for transfers between devices: 39.2 us -> 0.01 us  [local(): lax.all_gather(value_weight, 'req', axis=0, tiled=True)]
    all_gather x1 -> x0, waiting for transfers between devices: 33.5 us -> none  [fetch_adapters(): fetched = lax.all_gather(stored, 'req', axis=0, tiled=True)]
    all_gather x1, waiting for transfers between devices: 44.7 us -> 28.6 us  [local(): lax.all_gather(query_weight, 'req', axis=0, tiled=True)]
    concatenate x0 -> x2, local copies, waits for them, and re-layouts: none -> 3.43 us  [the longest x1 3.37 us: fetch_adapters(): jnp.roll(jnp.concatenate(ring[::-1], axis=0), (lax.axis_index('req') + 1)...]
    ppermute x0 -> x7, starting transfers between devices: none -> 3.03 us  [fetch_adapters(): lax.ppermute(ring[-1], 'req', [(dev, (dev + 1) % 8) for dev in range(8)])]
  transfers between devices with their start and end apart: 6 -> 12, of which waited for: 6 -> 11; matrix products, arithmetic and copies ran while one was open for 14% -> 15% of each run, Pallas kernels for 0% -> 0%
where the time goes in v1:
time: 266 us; the launch traced here: 265 us
  waiting for transfers between devices  195 us (73%)
  matrix products  31.7 us (12%)
  between operations  13.4 us (5%)
  local copies, waits for them, and re-layouts  8.23 us (3%)
  other arithmetic  8 us (3%)
  blocking collectives  5.64 us (2%)
  starting transfers between devices  3.23 us (1%)
    ppermute x7, waiting for transfers between devices, fetch_adapters(): lax.ppermute(ring[-1], 'req', [(dev, (dev + 1) % 8) for dev in range(8)])  56 us
    all_gather x1, waiting for transfers between devices, local(): lax.all_gather(key_weight, 'req', axis=0, tiled=True)  44.1 us
    all_gather x1, waiting for transfers between devices, local(): lax.all_gather(output_weight, 'req', axis=1, tiled=True)  34.7 us
    reduce_scatter x1, waiting for transfers between devices, local(): lax.psum_scatter(partial_out.astype(jnp.bfloat16), 'tp', scatter_dimensio...  29.8 us
    all_gather x1, waiting for transfers between devices, local(): lax.all_gather(query_weight, 'req', axis=0, tiled=True)  28.6 us
    sub x1, matrix products, attend(): scores - row_peak  8.19 us
    all_gather x1, blocking collectives, local(): shrunk = lax.all_gather(shrunk_part, 'tp', axis=1, tiled=True)  5.64 us
  transfers between devices with their start and end apart: 12, of which 11 were waited for; matrix products, arithmetic and copies ran while one was open for 15% of the time, Pallas kernels for 0%

profile of v1, /device:TPU:0, one launch (start us, length us, event | category | flops | bytes accessed | tf_op | source)
XLA Modules:
  0.0 265.4 jit_solution(17502435717379172334)
XLA Ops:
  10.0 3.0 %collective-permute-start = (bf16[2,32768]{1,0:T(2,128)(2,1)S(1)}, bf16[2,32768]{1,0:T(2,128)(2,1)S(1)}, u32[]{:S(2)}, u32[]{:S(2)}) collective-permute-start(bf16[2,32768]{1,0:T(2,128)(2,1)S(1)} %constant_dynamic-update-slice_fusion), channel_id=1, source_target_pairs={{0,4},{4,8},{8,12},{12,16},{16,20},{20,24},{24,28},{28,0},{1,5},{5... | collective-permute-start | bytes 393224 | tf_op jit(solution)/shard_map/ppermute | solution.py:19
  13.1 2.1 fusion.2
  17.6 1.9 collective-permute-done
  20.5 9.5 %collective-permute-done.1 = bf16[2,32768]{1,0:T(2,128)(2,1)S(1)} collective-permute-done((bf16[2,32768]{1,0:T(2,128)(2,1)S(1)}, bf16[2,32768]{1,0:T(2,128)(2,1)S(1)}, u32[]{:S(2)}, u32[]{:S(2)}) %collective-permute-start.1) | collective-permute-done | bytes 131104 | tf_op jit(solution)/shard_map/ppermute | solution.py:19
  30.1 8.4 %collective-permute-done.2 = bf16[2,32768]{1,0:T(2,128)(2,1)S(1)} collective-permute-done((bf16[2,32768]{1,0:T(2,128)(2,1)S(1)}, bf16[2,32768]{1,0:T(2,128)(2,1)S(1)}, u32[]{:S(2)}, u32[]{:S(2)}) %collective-permute-start.2) | collective-permute-done | bytes 131104 | tf_op jit(solution)/shard_map/ppermute | solution.py:19
  38.5 7.8 %collective-permute-done.3 = bf16[2,32768]{1,0:T(2,128)(2,1)S(1)} collective-permute-done((bf16[2,32768]{1,0:T(2,128)(2,1)S(1)}, bf16[2,32768]{1,0:T(2,128)(2,1)S(1)}, u32[]{:S(2)}, u32[]{:S(2)}) %collective-permute-start.3) | collective-permute-done | bytes 131104 | tf_op jit(solution)/shard_map/ppermute | solution.py:19
  46.3 11.1 %collective-permute-done.4 = bf16[2,32768]{1,0:T(2,128)(2,1)S(1)} collective-permute-done((bf16[2,32768]{1,0:T(2,128)(2,1)S(1)}, bf16[2,32768]{1,0:T(2,128)(2,1)S(1)}, u32[]{:S(2)}, u32[]{:S(2)}) %collective-permute-start.4) | collective-permute-done | bytes 131104 | tf_op jit(solution)/shard_map/ppermute | solution.py:19
  57.4 10.4 %collective-permute-done.5 = bf16[2,32768]{1,0:T(2,128)(2,1)S(1)} collective-permute-done((bf16[2,32768]{1,0:T(2,128)(2,1)S(1)}, bf16[2,32768]{1,0:T(2,128)(2,1)S(1)}, u32[]{:S(2)}, u32[]{:S(2)}) %collective-permute-start.5) | collective-permute-done | bytes 131104 | tf_op jit(solution)/shard_map/ppermute | solution.py:19
  68.6 6.9 %collective-permute-done.6 = bf16[2,32768]{1,0:T(2,128)(2,1)S(1)} collective-permute-done((bf16[2,32768]{1,0:T(2,128)(2,1)S(1)}, bf16[2,32768]{1,0:T(2,128)(2,1)S(1)}, u32[]{:S(2)}, u32[]{:S(2)}) %collective-permute-start.6) | collective-permute-done | bytes 131104 | tf_op jit(solution)/shard_map/ppermute | solution.py:19
  75.4 3.4 %concatenate.23 = bf16[32,32768]{1,0:T(8,128)(2,1)S(1)} concatenate(bf16[2,32768]{1,0:T(2,128)(2,1)S(1)} %collective-permute-done.6, bf16[2,32768]{1,0:T(2,128)(2,1)S(1)} %collective-permute-done.5, bf16[2,32768]{1,0:T(2,128)(2,1)S(1)} %collective-permute-done.4, bf16[2,32768]{1,0:T(2,128)(2,1)S(1)} %collective-permute-done.3, bf16[2,32768]{1,0:T(2,128)(2,1)S(1)} %collective-permute-done.2, ...), dimensions={0} | concatenate | bytes 4194304 | tf_op jit(solution)/shard_map/jit(_roll_dynamic)/concatenate | solution.py:20
  82.0 5.6 %all_gather.16 = bf16[512,32]{0,1:T(8,128)(2,1)S(1)} all-gather(bf16[512,8]{0,1:T(8,128)(2,1)S(1)} %fusion.17), channel_id=1, replica_groups=mesh['req'=8,'tp'=4] {'tp'}, dimensions={1}, use_global_device_ids=true | all-gather | bytes 40960 | tf_op jit(solution)/shard_map/all_gather | solution.py:155
  87.6 3.0 %fusion.68 = f32[512,512]{0,1:T(8,128)S(1)} fusion(bf16[2048,512]{1,0:T(8,128)(2,1)} %all-gather.5.cloned.1.call-done, bf16[512,2048]{1,0:T(8,128)(2,1)S(1)} %copy-done.2, f32[2048]{0:T(1024)S(1)} %convert_element_type.59, f32[512]{0:T(512)S(1)} %add_rsqrt_fusion), kind=kOutput, calls=%fused_computation.122 | convolution fusion | flops 1077936128 | bytes 5253120 | tf_op jit(solution)/shard_map/dot_general | solution.py:130
  90.6 2.3 fusion.12
  92.9 28.6 %all-gather.7.cloned.1.call-done = bf16[2048,512]{1,0:T(8,128)(2,1)} async-done(((bf16[256,512]{1,0:T(8,128)(2,1)}), bf16[2048,512]{1,0:T(8,128)(2,1)}) %all-gather.7.cloned.1.call-update) | async-done | bytes 2097168 | tf_op jit(solution)/shard_map/all_gather | solution.py:122
  121.5 3.9 %fusion.64 = f32[512,512]{0,1:T(8,128)} fusion(bf16[2048,512]{1,0:T(8,128)(2,1)} %all-gather.7.cloned.1.call-done, bf16[512,2048]{1,0:T(8,128)(2,1)S(1)} %copy-done.2, f32[2048]{0:T(1024)S(1)} %convert_element_type.59, f32[512]{0:T(512)S(1)} %add_rsqrt_fusion), kind=kOutput, calls=%fused_computation.121 | convolution fusion | flops 1077936128 | bytes 5253120 | tf_op jit(solution)/shard_map/dot_general | solution.py:120
  125.4 1.9 fusion.9
  127.3 44.1 %all-gather.9.cloned.1.call-done = bf16[2048,512]{1,0:T(8,128)(2,1)} async-done(((bf16[256,512]{1,0:T(8,128)(2,1)}), bf16[2048,512]{1,0:T(8,128)(2,1)}) %all-gather.9.cloned.1.call-update) | async-done | bytes 2097168 | tf_op jit(solution)/shard_map/all_gather | solution.py:127
  171.4 3.0 %fusion.62 = f32[512,512]{0,1:T(8,128)S(1)} fusion(bf16[2048,512]{1,0:T(8,128)(2,1)} %all-gather.9.cloned.1.call-done, bf16[512,2048]{1,0:T(8,128)(2,1)S(1)} %copy-done.2, f32[2048]{0:T(1024)S(1)} %convert_element_type.59, f32[512]{0:T(512)S(1)} %add_rsqrt_fusion), kind=kOutput, calls=%fused_computation.120 | convolution fusion | flops 1077936128 | bytes 5253120 | tf_op jit(solution)/shard_map/dot_general | solution.py:125
  175.7 8.2 %fusion.71 = (f32[8,512]{1,0:T(8,128)S(1)}, f32[8,512,512]{1,2,0:T(8,128)}) fusion(pred[512,512]{0,1:T(8,128)(4,1)} %fusion.18, bf16[512,8,32]{0,2,1:T(8,128)(2,1)} %get-tuple-element.13, bf16[512,8,32]{0,2,1:T(8,128)(2,1)} %get-tuple-element.14, bf16[512,8,32]{0,2,1:T(8,128)(2,1)} %get-tuple-element.8, bf16[512,8,32]{0,2,1:T(8,128)(2,1)} %get-tuple-element.7), kind=kOutput, calls=%fused_computation.124 | convolution fusion | flops 281018880 | bytes 9715712 | tf_op jit(solution)/shard_map/sub | solution.py:71
  183.9 4.2 %fusion.11 = bf16[8,64,512]{2,1,0:T(8,128)(2,1)S(1)} fusion(bf16[512,8,64]{0,2,1:T(8,128)(2,1)S(1)} %bitcast.44, f32[8,512,512]{1,2,0:T(8,128)} %get-tuple-element.18, f32[8,512]{1,0:T(8,128)S(1)} %get-tuple-element.17), kind=kOutput, calls=%fused_computation.21 | convolution fusion | flops 272891904 | bytes 9453568 | tf_op jit(solution)/shard_map/hqk,khd->qhd/dot_general | solution.py:73
  188.2 34.7 %all-gather.11.cloned.1.call-done = bf16[512,2048]{1,0:T(8,128)(2,1)} async-done(((bf16[512,256]{1,0:T(8,128)(2,1)}), bf16[512,2048]{1,0:T(8,128)(2,1)}) %all-gather.11.cloned.1.call-update) | async-done | bytes 2097168 | tf_op jit(solution)/shard_map/all_gather | solution.py:198
  222.9 4.2 %convolution_convert_fusion = bf16[512,2048]{1,0:T(8,128)(2,1)} fusion(bf16[512,512]{0,1:T(8,128)(2,1)S(1)} %bitcast.49, bf16[512,2048]{1,0:T(8,128)(2,1)} %all-gather.11.cloned.1.call-done), kind=kOutput, calls=%fused_computation.16 | convolution fusion | flops 1074790400 | bytes 4718592 | tf_op jit(solution)/shard_map/dot_general | solution.py:196
  227.1 29.8 %reduce-scatter.2.cloned.1.call-done = bf16[512,512]{1,0:T(8,128)(2,1)} async-done(((bf16[512,2048]{1,0:T(8,128)(2,1)}), bf16[512,512]{1,0:T(8,128)(2,1)}) %reduce-scatter.2.cloned.1.call-update) | async-done | bytes 524304 | tf_op jit(solution)/shard_map/reduce_scatter | solution.py:201
  256.9 2.0 add_convert_fusion
  (70 shorter events, 12.0 us)
Async XLA Ops:
  6.5 2.3 copy-start
  6.5 8.6 %copy-start.7 = (s32[1,8]{1,0:T(1,128)S(1)}, s32[1,8]{1,0:T(1,128)}, u32[]{:S(2)}) copy-start(s32[1,8]{1,0:T(1,128)} %param.14) | copy-start | bytes 100
  6.5 8.7 %copy-start.8 = (s32[16]{0:T(128)S(1)}, s32[16]{0:T(128)}, u32[]{:S(2)}) copy-start(s32[16]{0:T(128)} %param.15) | copy-start | bytes 196
  6.5 8.7 %copy-start.5 = (s32[1,512]{1,0:T(1,128)S(1)}, s32[1,512]{1,0:T(1,128)}, u32[]{:S(2)}) copy-start(s32[1,512]{1,0:T(1,128)} %param.13) | copy-start | bytes 6148
  6.5 10.4 %copy-start.1 = (s32[16]{0:T(128)S(1)}, s32[16]{0:T(128)}, u32[]{:S(2)}) copy-start(s32[16]{0:T(128)} %param.16) | copy-start | bytes 196
  6.5 81.1 %all-gather.5.cloned.1.call-start = ((), (), s32[]{:S(2)}) async-start(), calls=%async_computation.1 | async-start | bytes 2359296 | tf_op jit(solution)/shard_map/all_gather | solution.py:132
  7.3 114.2 %all-gather.7.cloned.1.call-start = ((), (), s32[]{:S(2)}) async-start(), calls=%async_computation.2 | async-start | bytes 2359296 | tf_op jit(solution)/shard_map/all_gather | solution.py:122
  8.0 59.8 %copy-start.6 = (bf16[2048]{0:T(1024)(128)(2,1)S(1)}, bf16[2048]{0:T(1024)(128)(2,1)}, u32[]{:S(2)}) copy-start(bf16[2048]{0:T(1024)(128)(2,1)} %param.17) | copy-start | bytes 12292
  8.0 163.4 %all-gather.9.cloned.1.call-start = ((), (), s32[]{:S(2)}) async-start(), calls=%async_computation.3 | async-start | bytes 2359296 | tf_op jit(solution)/shard_map/all_gather | solution.py:127
  8.8 214.1 %all-gather.11.cloned.1.call-start = ((), (), s32[]{:S(2)}) async-start(), calls=%async_computation.4 | async-start | bytes 2359296 | tf_op jit(solution)/shard_map/all_gather | solution.py:198
  10.0 9.6 %collective-permute-start = (bf16[2,32768]{1,0:T(2,128)(2,1)S(1)}, bf16[2,32768]{1,0:T(2,128)(2,1)S(1)}, u32[]{:S(2)}, u32[]{:S(2)}) collective-permute-start(bf16[2,32768]{1,0:T(2,128)(2,1)S(1)} %constant_dynamic-update-slice_fusion), channel_id=1, source_target_pairs={{0,4},{4,8},{8,12},{12,16},{16,20},{20,24},{24,28},{28,0},{1,5},{5... | collective-permute-start | bytes 393224 | tf_op jit(solution)/shard_map/ppermute | solution.py:19
  13.0 243.8 %reduce-scatter.2.cloned.1.call-start = ((), (), s32[]{:S(2)}) async-start(), calls=%async_computation.5 | async-start | bytes 2621440 | tf_op jit(solution)/shard_map/reduce_scatter | solution.py:201
  19.6 10.5 %collective-permute-start.1 = (bf16[2,32768]{1,0:T(2,128)(2,1)S(1)}, bf16[2,32768]{1,0:T(2,128)(2,1)S(1)}, u32[]{:S(2)}, u32[]{:S(2)}) collective-permute-start(bf16[2,32768]{1,0:T(2,128)(2,1)S(1)} %collective-permute-done), channel_id=1, source_target_pairs={{0,4},{4,8},{8,12},{12,16},{16,20},{20,24},{24,28},{28,0},{1,5},{5... | collective-permute-start | bytes 393224 | tf_op jit(solution)/shard_map/ppermute | solution.py:19
  30.0 8.4 %collective-permute-start.2 = (bf16[2,32768]{1,0:T(2,128)(2,1)S(1)}, bf16[2,32768]{1,0:T(2,128)(2,1)S(1)}, u32[]{:S(2)}, u32[]{:S(2)}) collective-permute-start(bf16[2,32768]{1,0:T(2,128)(2,1)S(1)} %collective-permute-done.1), channel_id=1, source_target_pairs={{0,4},{4,8},{8,12},{12,16},{16,20},{20,24},{24,28},{28,0},{1,5},{5... | collective-permute-start | bytes 393224 | tf_op jit(solution)/shard_map/ppermute | solution.py:19
  38.4 7.8 %collective-permute-start.3 = (bf16[2,32768]{1,0:T(2,128)(2,1)S(1)}, bf16[2,32768]{1,0:T(2,128)(2,1)S(1)}, u32[]{:S(2)}, u32[]{:S(2)}) collective-permute-start(bf16[2,32768]{1,0:T(2,128)(2,1)S(1)} %collective-permute-done.2), channel_id=1, source_target_pairs={{0,4},{4,8},{8,12},{12,16},{16,20},{20,24},{24,28},{28,0},{1,5},{5... | collective-permute-start | bytes 393224 | tf_op jit(solution)/shard_map/ppermute | solution.py:19
  46.3 11.2 %collective-permute-start.4 = (bf16[2,32768]{1,0:T(2,128)(2,1)S(1)}, bf16[2,32768]{1,0:T(2,128)(2,1)S(1)}, u32[]{:S(2)}, u32[]{:S(2)}) collective-permute-start(bf16[2,32768]{1,0:T(2,128)(2,1)S(1)} %collective-permute-done.3), channel_id=1, source_target_pairs={{0,4},{4,8},{8,12},{12,16},{16,20},{20,24},{24,28},{28,0},{1,5},{5... | collective-permute-start | bytes 393224 | tf_op jit(solution)/shard_map/ppermute | solution.py:19
  57.4 10.4 %collective-permute-start.5 = (bf16[2,32768]{1,0:T(2,128)(2,1)S(1)}, bf16[2,32768]{1,0:T(2,128)(2,1)S(1)}, u32[]{:S(2)}, u32[]{:S(2)}) collective-permute-start(bf16[2,32768]{1,0:T(2,128)(2,1)S(1)} %collective-permute-done.4), channel_id=1, source_target_pairs={{0,4},{4,8},{8,12},{12,16},{16,20},{20,24},{24,28},{28,0},{1,5},{5... | collective-permute-start | bytes 393224 | tf_op jit(solution)/shard_map/ppermute | solution.py:19
  67.8 7.7 %collective-permute-start.6 = (bf16[2,32768]{1,0:T(2,128)(2,1)S(1)}, bf16[2,32768]{1,0:T(2,128)(2,1)S(1)}, u32[]{:S(2)}, u32[]{:S(2)}) collective-permute-start(bf16[2,32768]{1,0:T(2,128)(2,1)S(1)} %collective-permute-done.5), channel_id=1, source_target_pairs={{0,4},{4,8},{8,12},{12,16},{16,20},{20,24},{24,28},{28,0},{1,5},{5... | collective-permute-start | bytes 393224 | tf_op jit(solution)/shard_map/ppermute | solution.py:19
  79.2 1.8 copy-start.2
  171.4 3.0 %copy-start.4 = (f32[512,32]{0,1:T(8,128)S(1)}, f32[512,32]{0,1:T(8,128)}, u32[]{:S(2)}) copy-start(f32[512,32]{0,1:T(8,128)} %get-tuple-element.16) | copy-start | bytes 196612
  175.7 8.2 %copy-start.3 = (bf16[512,512]{0,1:T(8,128)(2,1)S(1)}, bf16[512,512]{0,1:T(8,128)(2,1)}, u32[]{:S(2)}) copy-start(bf16[512,512]{0,1:T(8,128)(2,1)} %fusion.12) | copy-start | bytes 1572868
Sparse Core Ops, SparseCore 0:
  9.5 59.3 all-gather.4
  71.0 50.3 all-gather.6
  123.6 47.7 all-gather.8
  173.3 49.5 all-gather.10
  227.2 29.5 reduce-scatter.1
